TPU v7x, 512 devices: a whole 4x8x8 slice. The times are simulated.
512 devices in a mesh: seq: 64 (over y, z), tp: 8 (over x, core).
Axes of the slice: x: 4, y: 8, z: 8, core: 2. Of those that a mesh axis runs over, the one named last changes fastest.
Arguments:
- queries: bfloat16 [16384, 4096], P('seq', 'tp'), may hold values from -6 to 6
- keys: bfloat16 [16384, 4096], P('seq', 'tp'), may hold values from -6 to 6
- values: bfloat16 [16384, 4096], P('seq', 'tp'), may hold values from -6 to 6
- out_cotangent: bfloat16 [16384, 2048], P('seq', 'tp'), may hold values from -16 to 16
- proj_weight: bfloat16 [4096, 2048], P('tp', 'seq'), may hold values from -0.125 to 0.125
Outputs:
- grad_queries: bfloat16 [16384, 4096], P('seq', 'tp')
- grad_keys: bfloat16 [16384, 4096], P('seq', 'tp')
- grad_values: bfloat16 [16384, 4096], P('seq', 'tp')
- grad_proj: float32 [4096, 2048], P('tp', 'seq')
All inputs are finite; a program needn't handle non-finite values.
Results may differ from a plain program's by a relative error of at most 0.0058.
Values may be sent and summed in bfloat16 or wider, within the bound.
No kernel may reach another device: no remote copies, remote signals or barrier semaphores. Data moves between devices by JAX's collectives and lax.ppermute only.
A program may use at most 128 MiB of HBM per device.

v0:
```python
import jax
import jax.numpy as jnp
from jax import lax
from jax.sharding import PartitionSpec as P

DH = 128


def entering(part, axis, combine, identity, reverse):
    count = lax.axis_size(axis)
    place = lax.axis_index(axis)
    ahead = count - 1 - place if reverse else place
    gathered = lax.all_gather(part, axis)
    state = jnp.zeros_like(part) + jnp.asarray(identity, part.dtype)

    def one(step, state):
        source = count - 1 - step if reverse else step
        return combine(state, lax.dynamic_index_in_dim(gathered, source, 0, False))

    return lax.fori_loop(0, ahead, one, state)


def add_pair(earlier, later_one):
    return earlier + later_one


def per_device(queries, keys, values, out_cotangent, proj_weight):
    tok = queries.shape[0]
    heads = queries.shape[1] // DH
    seq_count = lax.axis_size("seq")
    scale = 1.0 / jnp.sqrt(jnp.float32(DH * tok * seq_count))
    q_heads = queries.reshape(tok, heads, DH)
    k_heads = keys.reshape(tok, heads, DH)
    v_heads = values.reshape(tok, heads, DH)
    kv_state = jnp.einsum("thd,the->hde", k_heads, v_heads, preferred_element_type=jnp.float32)
    zero_state = jnp.zeros_like(kv_state)
    prior_sum = entering(kv_state, "seq", add_pair, zero_state, False)
    full_cot = lax.all_gather(out_cotangent, "tp", axis=1, tiled=True)
    grad_out = lax.dot_general(
        full_cot,
        lax.all_gather(proj_weight, "seq", axis=1, tiled=True),
        (((1,), (1,)), ((), ())),
        preferred_element_type=jnp.float32,
    ).astype(jnp.bfloat16)
    g_heads = grad_out.reshape(tok, heads, DH)
    qg_state = jnp.einsum("thd,the->hde", q_heads, g_heads, preferred_element_type=jnp.float32)
    later_sum = entering(qg_state, "seq", add_pair, zero_state, True)
    prior = prior_sum.astype(jnp.bfloat16)
    later = later_sum.astype(jnp.bfloat16)
    rows = jnp.arange(tok)
    causal = (rows[:, None] >= rows[None, :])[None]
    attn = jnp.where(
        causal,
        jnp.einsum("thd,shd->hts", q_heads, k_heads, preferred_element_type=jnp.float32),
        0.0,
    ).astype(jnp.bfloat16)
    back = jnp.where(
        causal,
        jnp.einsum("thd,shd->hts", g_heads, v_heads, preferred_element_type=jnp.float32),
        0.0,
    ).astype(jnp.bfloat16)
    attn_out = scale * (
        jnp.einsum("hts,she->the", attn, v_heads, preferred_element_type=jnp.float32)
        + jnp.einsum("thd,hde->the", q_heads, prior, preferred_element_type=jnp.float32)
    )
    grad_q = scale * (
        jnp.einsum("hts,shd->thd", back, k_heads, preferred_element_type=jnp.float32)
        + jnp.einsum("the,hde->thd", g_heads, prior, preferred_element_type=jnp.float32)
    )
    grad_k = scale * (
        jnp.einsum("hts,thd->shd", back, q_heads, preferred_element_type=jnp.float32)
        + jnp.einsum("she,hde->shd", v_heads, later, preferred_element_type=jnp.float32)
    )
    grad_v = scale * (
        jnp.einsum("hts,the->she", attn, g_heads, preferred_element_type=jnp.float32)
        + jnp.einsum("shd,hde->she", k_heads, later, preferred_element_type=jnp.float32)
    )
    out_flat = attn_out.astype(jnp.bfloat16).reshape(tok, heads * DH)
    proj_term = lax.dot_general(
        out_flat, full_cot, (((0,), (0,)), ((), ())), preferred_element_type=jnp.float32
    )
    proj_sum = lax.psum_scatter(proj_term, "seq", scatter_dimension=1, tiled=True)
    grad_proj = proj_sum / jnp.sqrt(jnp.float32(tok * seq_count))
    width = heads * DH
    return (
        grad_q.astype(jnp.bfloat16).reshape(tok, width),
        grad_k.astype(jnp.bfloat16).reshape(tok, width),
        grad_v.astype(jnp.bfloat16).reshape(tok, width),
        grad_proj,
    )


def solution(mesh):
    return jax.shard_map(
        per_device,
        mesh=mesh,
        in_specs=(P("seq", "tp"), P("seq", "tp"), P("seq", "tp"), P("seq", "tp"), P("tp", "seq")),
        out_specs=(P("seq", "tp"), P("seq", "tp"), P("seq", "tp"), P("tp", "seq")),
        check_vma=False,
    )
```

profile of v0, /device:TPU:2, one launch (start us, length us, event | category | flops | bytes accessed | tf_op | source)
XLA Modules:
  0.0 670.4 jit_solution(11894771848935743379)
XLA Ops:
  8.7 1.1 copy.56
  9.8 1.9 fusion.17
  11.8 31.1 %all-gather.7.cloned.1.call-done = bf16[256,2048]{1,0:T(8,128)(2,1)} async-done(((bf16[256,256]{1,0:T(8,128)(2,1)}), bf16[256,2048]{1,0:T(8,128)(2,1)}) %all-gather.7.cloned.1.call-update) | async-done | bytes 1048592 | tf_op jit(solution)/shard_map/all_gather | solution.py:38
  42.9 88.4 %all-gather.9.cloned.1.call-done = bf16[512,2048]{0,1:T(8,128)(2,1)} async-done(((bf16[512,32]{0,1:T(8,128)(2,1)}), bf16[512,2048]{0,1:T(8,128)(2,1)}) %all-gather.9.cloned.1.call-update) | async-done | bytes 2097168 | tf_op jit(solution)/shard_map/all_gather | solution.py:41
  131.3 2.6 convolution_convert_fusion
  135.9 135.8 %all-gather.11.cloned.1.call-done = f32[256,128,128]{2,1,0:T(8,128)} async-done(((f32[4,128,128]{2,1,0:T(8,128)}), f32[256,128,128]{2,1,0:T(8,128)}) %all-gather.11.cloned.1.call-update) | async-done | bytes 16777232 | tf_op jit(solution)/shard_map/all_gather | solution.py:13
  272.1 2.7 fusion.35
  277.1 136.3 %all-gather.13.cloned.1.call-done = f32[256,128,128]{2,1,0:T(8,128)} async-done(((f32[4,128,128]{2,1,0:T(8,128)}), f32[256,128,128]{2,1,0:T(8,128)}) %all-gather.13.cloned.1.call-update) | async-done | bytes 16777232 | tf_op jit(solution)/shard_map/all_gather | solution.py:13
  413.4 65.1 %while.23 = (s32[]{:T(128)}, f32[4,128,128]{2,1,0:T(8,128)S(1)}, s32[]{:T(128)}, f32[64,4,128,128]{3,2,1,0:T(8,128)}, s32[]{:T(128)}, /*index=5*/s32[]{:T(128)}, s32[]{:T(128)}, s32[]{:T(128)}) while((s32[]{:T(128)}, f32[4,128,128]{2,1,0:T(8,128)S(1)}, s32[]{:T(128)}, f32[64,4,128,128]{3,2,1,0:T(8,128)}, s32[]{:T(128)}, /*index=5*/s32[]{:T(128)}, ...), condition=%wide.region_3.4_spmd, body=%wide.region_2.3_spmd.sunk | while | flops 65542 | bytes 786575 | solution.py:20
  429.9 1.0 bitcast_add_fusion.5
  435.1 1.0 bitcast_add_fusion.5
  436.1 1.0 bitcast_add_fusion.5
  440.3 1.0 bitcast_add_fusion.5
  441.3 1.0 bitcast_add_fusion.5
  443.4 1.0 bitcast_add_fusion.5
  446.5 1.0 bitcast_add_fusion.5
  447.5 1.0 bitcast_add_fusion.5
  449.6 1.0 bitcast_add_fusion.5
  453.7 1.0 bitcast_add_fusion.5
  456.8 1.0 bitcast_add_fusion.5
  457.9 1.0 bitcast_add_fusion.5
  461.0 1.0 bitcast_add_fusion.5
  464.1 1.0 bitcast_add_fusion.5
  465.1 1.0 bitcast_add_fusion.5
  467.2 1.0 bitcast_add_fusion.5
  471.3 1.0 bitcast_add_fusion.5
  473.4 1.0 bitcast_add_fusion.5
  474.4 1.0 bitcast_add_fusion.5
  476.5 1.0 bitcast_add_fusion.5
  477.5 1.0 bitcast_add_fusion.5
  480.7 181.7 %reduce-scatter.2.cloned.1.call-done = f32[512,32]{0,1:T(8,128)} async-done(((f32[512,2048]{0,1:T(8,128)}), f32[512,32]{0,1:T(8,128)}) %reduce-scatter.2.cloned.1.call-update) | async-done | bytes 65552 | tf_op jit(solution)/shard_map/reduce_scatter | solution.py:82
  662.4 1.5 broadcast_multiply_fusion
  (78 shorter events, 50.6 us)
Async XLA Ops:
  7.2 126.9 %copy-start = (bf16[256,512]{1,0:T(8,128)(2,1)S(1)}, bf16[256,512]{1,0:T(8,128)(2,1)}, u32[]{:S(2)}) copy-start(bf16[256,512]{1,0:T(8,128)(2,1)} %param.9) | copy-start | bytes 786436
  7.2 128.1 %copy-start.1 = (bf16[256,512]{1,0:T(8,128)(2,1)S(1)}, bf16[256,512]{1,0:T(8,128)(2,1)}, u32[]{:S(2)}) copy-start(bf16[256,512]{1,0:T(8,128)(2,1)} %param.10) | copy-start | bytes 786436
  7.2 35.7 %all-gather.7.cloned.1.call-start = ((), (), s32[]{:S(2)}) async-start(), calls=%async_computation.1 | async-start | bytes 1179648 | tf_op jit(solution)/shard_map/all_gather | solution.py:38
  7.9 123.4 %all-gather.9.cloned.1.call-start = ((), (), s32[]{:S(2)}) async-start(), calls=%async_computation.2 | async-start | bytes 2129920 | tf_op jit(solution)/shard_map/all_gather | solution.py:41
  8.7 263.1 %all-gather.11.cloned.1.call-start = ((), (), s32[]{:S(2)}) async-start(), calls=%async_computation.4 | async-start | bytes 17039360 | tf_op jit(solution)/shard_map/all_gather | solution.py:13
  11.8 401.6 %all-gather.13.cloned.1.call-start = ((), (), s32[]{:S(2)}) async-start(), calls=%async_computation.5 | async-start | bytes 17039360 | tf_op jit(solution)/shard_map/all_gather | solution.py:13
  135.2 527.2 %reduce-scatter.2.cloned.1.call-start = ((), (), s32[]{:S(2)}) async-start(), calls=%async_computation.3 | async-start | bytes 4259840 | tf_op jit(solution)/shard_map/reduce_scatter | solution.py:82
  135.3 136.8 %copy-start.2 = (bf16[256,2048]{1,0:T(8,128)(2,1)S(1)}, bf16[256,2048]{1,0:T(8,128)(2,1)}, u32[]{:S(2)}) copy-start(bf16[256,2048]{1,0:T(8,128)(2,1)} %all-gather.7.cloned.1.call-done) | copy-start | bytes 3145732
Sparse Core Ops, SparseCore 0:
  10.1 32.7 all-gather.6
  45.9 85.3 all-gather.8
  134.9 136.7 all-gather.10
  275.2 138.1 all-gather.12
  417.3 245.0 reduce-scatter.1
where the time goes:
time: 673 us; the launch traced here: 670 us
  waiting for transfers between devices  575 us (85%)
  other arithmetic  65.2 us (10%)
  between operations  13.9 us (2%)
  matrix products  10.2 us (2%)
    all_gather x2, waiting for transfers between devices, entering(): gathered = lax.all_gather(part, axis)  272 us
    reduce_scatter x1, waiting for transfers between devices, per_device(): lax.psum_scatter(proj_term, 'seq', scatter_dimension=1, tiled=True)  182 us
    all_gather x1, waiting for transfers between devices, per_device(): lax.all_gather(proj_weight, 'seq', axis=1, tiled=True)  88.4 us
    add x63, other arithmetic, add_pair(): return earlier + later_one  63.7 us
    all_gather x1, waiting for transfers between devices, per_device(): full_cot = lax.all_gather(out_cotangent, 'tp', axis=1, tiled=True)  31.1 us
  transfers between devices with their start and end apart: 5, of which 5 were waited for; matrix products, arithmetic and copies ran while one was open for 12% of the time, Pallas kernels for 0%

commit v1 on v0

--- a/solution.py
+++ b/solution.py
@@ -4,6 +4,21 @@
 from jax.sharding import PartitionSpec as P
 
 DH = 128
+
+
+def save_routes_all(obj, which_axis, axis_k):
+    n_slots = lax.axis_size(which_axis)
+    plain = sorted(((q, (q + 1) % n_slots) for q in range(n_slots)))
+    upper = obj
+    idx = 1
+    crops = [upper]
+    while idx < n_slots:
+        upper = lax.ppermute(upper, which_axis, plain)
+        crops.insert(0, upper)
+        idx = idx + 1
+    shaped = jnp.concatenate(crops, axis=axis_k)
+    inter = lax.axis_index(which_axis) + 1
+    return jnp.roll(shaped, inter * obj.shape[axis_k], axis=axis_k)
 
 
 def entering(part, axis, combine, identity, reverse):
@@ -35,7 +50,7 @@
     kv_state = jnp.einsum("thd,the->hde", k_heads, v_heads, preferred_element_type=jnp.float32)
     zero_state = jnp.zeros_like(kv_state)
     prior_sum = entering(kv_state, "seq", add_pair, zero_state, False)
-    full_cot = lax.all_gather(out_cotangent, "tp", axis=1, tiled=True)
+    full_cot = save_routes_all(out_cotangent, "tp", 1)
     grad_out = lax.dot_general(
         full_cot,
         lax.all_gather(proj_weight, "seq", axis=1, tiled=True),

time: 673 us -> 641 us (0.952)
  the two profiles are of different devices: /device:TPU:2 before, /device:TPU:4 now
where the time goes in v1:
time: 641 us; the launch traced here: 639 us
  waiting for transfers between devices  536 us (84%)
  other arithmetic  65.2 us (10%)
  between operations  14.1 us (2%)
  matrix products  11.1 us (2%)
  local copies, waits for them, and re-layouts  6.63 us (1%)
    all_gather x2, waiting for transfers between devices, entering(): gathered = lax.all_gather(part, axis)  271 us
    reduce_scatter x1, waiting for transfers between devices, per_device(): lax.psum_scatter(proj_term, 'seq', scatter_dimension=1, tiled=True)  182 us
    add x63, other arithmetic, add_pair(): return earlier + later_one  63.7 us
    all_gather x1, waiting for transfers between devices, per_device(): lax.all_gather(proj_weight, 'seq', axis=1, tiled=True)  55.1 us
    ppermute x7, waiting for transfers between devices, save_routes_all(): upper = lax.ppermute(upper, which_axis, plain)  26.8 us
  transfers between devices with their start and end apart: 11, of which 11 were waited for; matrix products, arithmetic and copies ran while one was open for 13% of the time, Pallas kernels for 0%

profile of v1, /device:TPU:4, one launch (start us, length us, event | category | flops | bytes accessed | tf_op | source)
XLA Modules:
  0.0 638.8 jit_solution(16174519634430709755)
XLA Ops:
  8.0 1.1 copy.56
  9.1 1.9 fusion.20
  11.1 4.6 collective-permute-done
  15.7 4.4 collective-permute-done.1
  20.1 4.4 collective-permute-done.2
  24.5 4.4 collective-permute-done.3
  29.1 4.2 collective-permute-done.4
  33.3 1.4 collective-permute-start.5
  34.7 3.0 collective-permute-done.5
  37.7 2.6 collective-permute-start.6
  40.3 1.9 collective-permute-done.6
  44.3 55.1 %all-gather.6.cloned.1.call-done = bf16[512,2048]{0,1:T(8,128)(2,1)} async-done(((bf16[512,32]{0,1:T(8,128)(2,1)}), bf16[512,2048]{0,1:T(8,128)(2,1)}) %all-gather.6.cloned.1.call-update) | async-done | bytes 2097168 | tf_op jit(solution)/shard_map/all_gather | solution.py:56
  99.4 2.3 convolution_convert_fusion
  103.7 136.1 %all-gather.8.cloned.1.call-done = f32[256,128,128]{2,1,0:T(8,128)} async-done(((f32[4,128,128]{2,1,0:T(8,128)}), f32[256,128,128]{2,1,0:T(8,128)}) %all-gather.8.cloned.1.call-update) | async-done | bytes 16777232 | tf_op jit(solution)/shard_map/all_gather | solution.py:28
  240.1 3.9 fusion.13
  246.4 135.2 %all-gather.10.cloned.1.call-done = f32[256,128,128]{2,1,0:T(8,128)} async-done(((f32[4,128,128]{2,1,0:T(8,128)}), f32[256,128,128]{2,1,0:T(8,128)}) %all-gather.10.cloned.1.call-update) | async-done | bytes 16777232 | tf_op jit(solution)/shard_map/all_gather | solution.py:28
  381.6 65.4 %while.23 = (s32[]{:T(128)}, f32[4,128,128]{2,1,0:T(8,128)S(1)}, s32[]{:T(128)}, f32[64,4,128,128]{3,2,1,0:T(8,128)}, s32[]{:T(128)}, /*index=5*/s32[]{:T(128)}, s32[]{:T(128)}, s32[]{:T(128)}) while((s32[]{:T(128)}, f32[4,128,128]{2,1,0:T(8,128)S(1)}, s32[]{:T(128)}, f32[64,4,128,128]{3,2,1,0:T(8,128)}, s32[]{:T(128)}, /*index=5*/s32[]{:T(128)}, ...), condition=%wide.region_3.4_spmd, body=%wide.region_2.3_spmd.sunk | while | flops 65542 | bytes 786567 | solution.py:35
  398.2 1.0 bitcast_add_fusion.5
  404.5 1.0 bitcast_add_fusion.5
  408.6 1.0 bitcast_add_fusion.5
  409.7 1.0 bitcast_add_fusion.5
  411.7 1.0 bitcast_add_fusion.5
  414.8 1.0 bitcast_add_fusion.5
  415.9 1.0 bitcast_add_fusion.5
  418.0 1.0 bitcast_add_fusion.5
  422.1 1.0 bitcast_add_fusion.5
  424.2 1.0 bitcast_add_fusion.5
  425.2 1.0 bitcast_add_fusion.5
  428.4 1.0 bitcast_add_fusion.5
  445.0 1.0 bitcast_add_fusion.5
  449.2 181.5 %reduce-scatter.2.cloned.1.call-done = f32[512,32]{0,1:T(8,128)} async-done(((f32[512,2048]{0,1:T(8,128)}), f32[512,32]{0,1:T(8,128)}) %reduce-scatter.2.cloned.1.call-update) | async-done | bytes 65552 | tf_op jit(solution)/shard_map/reduce_scatter | solution.py:97
  630.8 1.5 broadcast_multiply_fusion
  (107 shorter events, 60.2 us)
Async XLA Ops:
  7.2 94.7 %copy-start = (bf16[256,512]{1,0:T(8,128)(2,1)S(1)}, bf16[256,512]{1,0:T(8,128)(2,1)}, u32[]{:S(2)}) copy-start(bf16[256,512]{1,0:T(8,128)(2,1)} %param.9) | copy-start | bytes 786436
  7.2 36.0 %copy-start.3 = (bf16[256,256]{1,0:T(8,128)(2,1)S(1)}, bf16[256,256]{1,0:T(8,128)(2,1)}, u32[]{:S(2)}) copy-start(bf16[256,256]{1,0:T(8,128)(2,1)} %param.12) | copy-start | bytes 393220
  7.2 92.2 %all-gather.6.cloned.1.call-start = ((), (), s32[]{:S(2)}) async-start(), calls=%async_computation.1 | async-start | bytes 2129920 | tf_op jit(solution)/shard_map/all_gather | solution.py:56
  7.9 231.9 %all-gather.8.cloned.1.call-start = ((), (), s32[]{:S(2)}) async-start(), calls=%async_computation.3 | async-start | bytes 17039360 | tf_op jit(solution)/shard_map/all_gather | solution.py:28
  11.0 370.6 %all-gather.10.cloned.1.call-start = ((), (), s32[]{:S(2)}) async-start(), calls=%async_computation.4 | async-start | bytes 17039360 | tf_op jit(solution)/shard_map/all_gather | solution.py:28
  11.1 4.6 collective-permute-start
  15.7 4.4 collective-permute-start.1
  20.1 4.4 collective-permute-start.2
  24.5 4.4 collective-permute-start.3
  28.9 4.4 collective-permute-start.4
  33.3 4.4 collective-permute-start.5
  37.7 4.5 collective-permute-start.6
  44.3 55.2 %copy-start.2 = (bf16[256,4096]{1,0:T(8,128)(2,1)}, bf16[256,4096]{1,0:T(8,128)(2,1)S(1)}, u32[]{:S(2)}) copy-start(bf16[256,4096]{1,0:T(8,128)(2,1)S(1)} %constant_dynamic-update-slice_fusion) | copy-start | bytes 6291460
  44.3 58.8 %copy-start.1 = (bf16[256,512]{1,0:T(8,128)(2,1)S(1)}, bf16[256,512]{1,0:T(8,128)(2,1)}, u32[]{:S(2)}) copy-start(bf16[256,512]{1,0:T(8,128)(2,1)} %param.10) | copy-start | bytes 786436
  103.0 527.8 %reduce-scatter.2.cloned.1.call-start = ((), (), s32[]{:S(2)}) async-start(), calls=%async_computation.2 | async-start | bytes 4259840 | tf_op jit(solution)/shard_map/reduce_scatter | solution.py:97
Sparse Core Ops, SparseCore 0:
  11.0 88.3 all-gather.5
  103.0 136.7 all-gather.7
  243.4 138.1 all-gather.9
  385.5 245.2 reduce-scatter.1
